TPU v7x, 256 devices: a whole 4x4x8 slice. The times are simulated.
256 devices in a mesh: srv: 8 (over y, core), head: 4 (over x), wsh: 8 (over z).
Axes of the slice: x: 4, y: 4, z: 8, core: 2. Of those that a mesh axis runs over, the one named last changes fastest.
Arguments:
- queries: bfloat16 [12288, 8192], P(('srv', 'wsh'), 'head'), may hold values from -4.5 to 4.5
- keys: bfloat16 [12288, 1024], P(('srv', 'wsh'), 'head'), may hold values from -4.5 to 4.5
- values: bfloat16 [12288, 1024], P(('srv', 'wsh'), 'head'), may hold values from -6 to 6
- doc_ids: int32 [12288], replicated, may hold values from 0 to 2, never falling along the last dimension, each value on 1 to 11904 neighbouring positions
- block_mask: int32 [64, 4], replicated, may hold values from 0 to 1, as said below
- out_weight: bfloat16 [8192, 8192], P(('head', 'wsh')), may hold values from -0.0625 to 0.0625
Outputs:
- projected: bfloat16 [12288, 8192], P(('srv', 'head', 'wsh'))
Inputs may be any that keep to these rules, and one draw needn't show every extreme that they name: `block_mask`: column 0 is 1 in every row; other entries are 0 or 1.
All inputs are finite; a program needn't handle non-finite values.
Results may differ from a plain program's by a relative error of at most 0.017.
Values may be sent and summed in bfloat16 or wider, within the bound.
A program may use at most 128 MiB of HBM per device.

v0:
```python
from functools import partial
import math

import jax
import jax.numpy as jnp
from jax import lax
from jax.sharding import PartitionSpec as P

QUERY_HEAD_COUNT = 64
KEY_VALUE_HEADS = 8
HEAD_SIZE = 128
SLAB_REACH = 4


floor_score = -1e30


def shifted(block, axis, distance):
    devices = range(lax.axis_size(axis))
    route = [(i - distance, i) for i in devices if i - distance in devices]
    return lax.ppermute(block, axis, route)


def tile_update(carried, query_heads, key_block, value_block, docs_query, docs_key, causal):
    running_max, running_sum, weighted = carried
    row_count = query_heads.shape[0]
    key_heads = key_block.reshape(row_count, -1, HEAD_SIZE)
    value_heads = value_block.reshape(row_count, -1, HEAD_SIZE)
    scores = jnp.einsum(
        "qhgd,khd->hgqk", query_heads, key_heads, preferred_element_type=jnp.float32
    ) * (1.0 / math.sqrt(HEAD_SIZE))
    visible = docs_query[:, None] == docs_key[None, :]
    if causal:
        query_pos = lax.broadcasted_iota(jnp.int32, (row_count, row_count), 0)
        key_pos = lax.broadcasted_iota(jnp.int32, (row_count, row_count), 1)
        visible = visible & (key_pos <= query_pos)
    masked = jnp.where(visible, scores, floor_score)
    freshest = jnp.maximum(running_max, jnp.max(masked, axis=-1))
    softmax_terms = jnp.where(visible, jnp.exp(masked - freshest[..., None]), 0.0)
    rescale = jnp.exp(running_max - freshest)
    running_sum = running_sum * rescale + jnp.sum(softmax_terms, axis=-1)
    update = jnp.einsum(
        "hgqk,khd->qhgd",
        softmax_terms.astype(jnp.bfloat16),
        value_heads,
        preferred_element_type=jnp.float32,
    )
    weighted = weighted * jnp.transpose(rescale, (2, 0, 1))[..., None] + update
    return (freshest, running_sum, weighted)


def on_device(queries, keys, values, doc_ids, block_mask, out_weight):
    row_count = queries.shape[0]
    kv_local = keys.shape[1] // HEAD_SIZE
    query_group_width = QUERY_HEAD_COUNT // KEY_VALUE_HEADS
    query_heads = queries.reshape(row_count, kv_local, query_group_width, HEAD_SIZE)
    current_slab = lax.axis_index(("srv", "wsh"))
    docs_query = lax.dynamic_slice_in_dim(doc_ids, current_slab * row_count, row_count)
    mask_row = lax.dynamic_index_in_dim(block_mask, current_slab, 0, keepdims=False)
    carried = (
        jnp.full((kv_local, query_group_width, row_count), floor_score, jnp.float32),
        jnp.zeros((kv_local, query_group_width, row_count), jnp.float32),
        jnp.zeros((row_count, kv_local, query_group_width, HEAD_SIZE), jnp.float32),
    )
    for offset in range(SLAB_REACH):
        if offset == 0:
            key_block, value_block = (keys, values)
        else:
            key_block, value_block = shifted((keys, values), ("srv", "wsh"), offset)
        source = current_slab - offset
        docs_key = lax.dynamic_slice_in_dim(doc_ids, jnp.maximum(source, 0) * row_count, row_count)
        live = (mask_row[offset] > 0) & (source >= 0)
        update_tile = partial(
            tile_update,
            query_heads=query_heads,
            key_block=key_block,
            value_block=value_block,
            docs_query=docs_query,
            docs_key=docs_key,
            causal=offset == 0,
        )
        carried = lax.cond(live, update_tile, lambda running: running, carried)
    running_max, running_sum, weighted = carried
    normalizer = jnp.transpose(running_sum, (2, 0, 1))[..., None]
    attention = (weighted / normalizer).reshape(row_count, -1).astype(jnp.bfloat16)
    spread = lax.all_to_all(attention, "wsh", split_axis=1, concat_axis=0, tiled=True)
    return lax.psum_scatter(
        jnp.dot(spread, out_weight, preferred_element_type=jnp.float32).astype(jnp.bfloat16),
        ("head", "wsh"),
        scatter_dimension=0,
        tiled=True,
    )


def solution(mesh):
    in_specs = (
        P(("srv", "wsh"), "head"),
        P(("srv", "wsh"), "head"),
        P(("srv", "wsh"), "head"),
        P(),
        P(),
        P(("head", "wsh"), None),
    )
    out_specs = P(("srv", "head", "wsh"), None)
    return jax.shard_map(
        on_device, mesh=mesh, in_specs=in_specs, out_specs=out_specs, check_vma=False
    )
```

profile of v0, /device:TPU:8, one launch (start us, length us, event | category | flops | bytes accessed | tf_op | source)
XLA Modules:
  0.0 376.3 jit_solution(4070526298708555387)
XLA Ops:
  6.5 3.9 %collective-permute-start = (bf16[192,256]{1,0:T(8,128)(2,1)}, bf16[192,256]{1,0:T(8,128)(2,1)S(1)}, u32[]{:S(2)}, u32[]{:S(2)}) collective-permute-start(bf16[192,256]{1,0:T(8,128)(2,1)} %param.15), channel_id=1, source_target_pairs={{0,1},{1,2},{2,3},{3,4},{4,5},{5,6},{6,7},{7,32},{32,33},{33,34},{... | collective-permute-start | bytes 294920 | tf_op jit(solution)/shard_map/ppermute | solution.py:21
  10.5 7.7 %collective-permute-start.4 = (bf16[192,256]{1,0:T(8,128)(2,1)}, bf16[192,256]{1,0:T(8,128)(2,1)S(1)}, u32[]{:S(2)}, u32[]{:S(2)}) collective-permute-start(bf16[192,256]{1,0:T(8,128)(2,1)} %param.15), channel_id=1, source_target_pairs={{0,3},{1,4},{2,5},{3,6},{4,7},{5,32},{6,33},{7,34},{32,35},{33,36}... | collective-permute-start | bytes 294920 | tf_op jit(solution)/shard_map/ppermute | solution.py:21
  18.2 3.4 collective-permute-start.2
  21.6 2.9 collective-permute-start.1
  24.6 1.9 collective-permute-start.5
  26.6 0.6 fusion.83
  29.8 1.3 copy.83
  31.1 5.3 %collective-permute-start.3 = (bf16[192,256]{1,0:T(8,128)(2,1)}, bf16[192,256]{1,0:T(8,128)(2,1)S(1)}, u32[]{:S(2)}, u32[]{:S(2)}) collective-permute-start(bf16[192,256]{1,0:T(8,128)(2,1)} %param.16), channel_id=1, source_target_pairs={{0,2},{1,3},{2,4},{3,5},{4,6},{5,7},{6,32},{7,33},{32,34},{33,35},... | collective-permute-start | bytes 294920 | tf_op jit(solution)/shard_map/ppermute | solution.py:21
  36.4 0.9 fusion.82
  37.3 7.7 %conditional.4 = (f32[2,8,192]{2,1,0:T(8,128)}, f32[2,8,192]{2,1,0:T(8,128)S(1)}, f32[192,2,8,128]{3,0,2,1:T(8,128)S(1)}) conditional(s32[]{:T(128)} %convert_element_type.39, () %tuple.38, (s32[192]{0:T(256)S(1)}, s32[192]{0:T(256)S(1)}, bf16[192,256]{1,0:T(8,128)(2,1)}, bf16[192,2,8,128]{3,2,1,0:T(8,128)(2,1)S(1)}, bf16[192,256]{1,0:T(8,128)(2,1)}) %tuple.81), branch_computations={%region_0.1_spmd, %region_1.4_spmd} | conditional | flops 310173696 | bytes 10311192 | solution.py:82
  37.4 0.9 reshape.64
  38.3 0.9 reshape.63
  39.3 0.8 fusion
  40.1 0.6 fusion.17
  40.7 1.5 fusion.2
  42.2 2.1 bitcast_add_fusion
  44.3 0.7 fusion.18
  45.0 5.5 %conditional.5 = ((f32[2,8,192]{2,1,0:T(8,128)}, f32[2,8,192]{2,1,0:T(8,128)S(1)}, f32[192,2,8,128]{3,0,2,1:T(8,128)S(1)})) conditional(s32[]{:T(128)} %convert_element_type.38, (f32[2,8,192]{2,1,0:T(8,128)}, f32[2,8,192]{2,1,0:T(8,128)S(1)}, f32[192,2,8,128]{3,0,2,1:T(8,128)S(1)}) %conditional.4, (s32[192]{0:T(256)S(1)}, s32[192]{0:T(256)S(1)}, ...), branch_computations={%region_4.5_spmd, %region_5.8_spmd} | conditional | flops 310490112 | bytes 11945504 | solution.py:82
  45.2 0.8 fusion.22
  46.0 0.7 fusion.38
  46.8 1.6 bitcast_add_fusion.1
  48.4 0.8 fusion.24
  49.2 0.7 multiply_add_fusion
  49.9 0.6 copy.133
  50.6 6.3 %conditional.6 = ((f32[2,8,192]{2,1,0:T(8,128)}, f32[2,8,192]{2,1,0:T(8,128)S(1)}, f32[192,2,8,128]{3,0,2,1:T(8,128)S(1)})) conditional(s32[]{:T(128)} %convert_element_type.37, (f32[2,8,192]{2,1,0:T(8,128)}, f32[2,8,192]{2,1,0:T(8,128)S(1)}, f32[192,2,8,128]{3,0,2,1:T(8,128)S(1)}) %get-tuple-element.317, (s32[192]{0:T(256)S(1)}, s32[]{:T(128)}, ...), branch_computations={%region_8.9_spmd, %region_9.12_spmd} | conditional | flops 310490112 | bytes 11947102 | solution.py:82
  50.6 0.8 dynamic_slice.17
  51.4 0.1 broadcast_compare_fusion.1
  51.5 0.8 fusion.42
  52.3 0.7 fusion.58
  53.0 1.6 bitcast_add_fusion.2
  54.7 0.8 fusion.44
  55.5 0.7 multiply_add_fusion.1
  56.2 0.6 copy.139
  56.8 5.7 %conditional.7 = ((f32[2,8,192]{2,1,0:T(8,128)S(1)}, f32[192,2,8,128]{3,0,2,1:T(8,128)S(1)})) conditional(s32[]{:T(128)} %convert_element_type.36, (f32[2,8,192]{2,1,0:T(8,128)S(1)}, f32[192,2,8,128]{3,0,2,1:T(8,128)S(1)}) %tuple.42, (s32[192]{0:T(256)S(1)}, s32[]{:T(128)}, s32[12288]{0:T(1024)}, bf16[192,256]{1,0:T(8,128)(2,1)S(1)}, ...), branch_computations={%region_12.13_spmd, %region_13.16_spmd} | conditional | flops 310490112 | bytes 11922518 | solution.py:82
  56.9 0.8 dynamic_slice.18
  57.6 0.1 broadcast_compare_fusion.2
  57.8 0.8 fusion.62
  58.6 0.7 fusion.78
  59.3 1.6 bitcast_add_fusion.3
  60.9 0.8 fusion.64
  61.8 0.7 multiply_add_fusion.2
  62.5 0.5 divide_convert_fusion
  63.0 0.5 copy.53
  63.5 0.3 convert_element_type.41
  63.8 0.2 copy.54
  63.9 26.9 %all_to_all.16 = bf16[192,8,256]{2,0,1:T(8,128)(2,1)S(1)} all-to-all(bf16[192,8,256]{2,0,1:T(8,128)(2,1)S(1)} %copy.54), channel_id=1, replica_groups=mesh['srv'=8,'head'=4,'wsh'=8] {'wsh'}, dimensions={1} | all-to-all | bytes 1572864 | tf_op jit(solution)/shard_map/all_to_all | solution.py:86
  90.9 13.9 %convolution_convert_fusion = bf16[1536,8192]{1,0:T(8,128)(2,1)} fusion(bf16[1536,256]{1,0:T(8,128)(2,1)S(1)} %bitcast.95, bf16[256,8192]{1,0:T(8,128)(2,1)} %param.19), kind=kOutput, calls=%fused_computation.94 | convolution fusion | flops 6455033856 | bytes 30146560 | tf_op jit(solution)/shard_map/dot_general | solution.py:88
  104.8 264.7 %reduce-scatter.2.cloned.1.call-done = bf16[48,8192]{1,0:T(8,128)(2,1)} async-done(((bf16[1536,8192]{1,0:T(8,128)(2,1)}), bf16[48,8192]{1,0:T(8,128)(2,1)}) %reduce-scatter.2.cloned.1.call-update) | async-done | bytes 786448 | tf_op jit(solution)/shard_map/reduce_scatter | solution.py:87
  (19 shorter events, 0.5 us)
Async XLA Ops:
  6.5 20.0 %copy-start = (s32[64,4]{0,1:T(4,128)S(1)}, s32[64,4]{0,1:T(4,128)}, u32[]{:S(2)}) copy-start(s32[64,4]{0,1:T(4,128)} %param.18) | copy-start | bytes 3076
  6.5 362.9 %reduce-scatter.2.cloned.1.call-start = ((), (), s32[]{:S(2)}) async-start(), calls=%async_computation.2 | async-start | bytes 25952256 | tf_op jit(solution)/shard_map/reduce_scatter | solution.py:87
  6.5 24.5 %collective-permute-start = (bf16[192,256]{1,0:T(8,128)(2,1)}, bf16[192,256]{1,0:T(8,128)(2,1)S(1)}, u32[]{:S(2)}, u32[]{:S(2)}) collective-permute-start(bf16[192,256]{1,0:T(8,128)(2,1)} %param.15), channel_id=1, source_target_pairs={{0,1},{1,2},{2,3},{3,4},{4,5},{5,6},{6,7},{7,32},{32,33},{33,34},{... | collective-permute-start | bytes 294920 | tf_op jit(solution)/shard_map/ppermute | solution.py:21
  10.5 46.3 %collective-permute-start.4 = (bf16[192,256]{1,0:T(8,128)(2,1)}, bf16[192,256]{1,0:T(8,128)(2,1)S(1)}, u32[]{:S(2)}, u32[]{:S(2)}) collective-permute-start(bf16[192,256]{1,0:T(8,128)(2,1)} %param.15), channel_id=1, source_target_pairs={{0,3},{1,4},{2,5},{3,6},{4,7},{5,32},{6,33},{7,34},{32,35},{33,36}... | collective-permute-start | bytes 294920 | tf_op jit(solution)/shard_map/ppermute | solution.py:21
  18.2 32.3 %collective-permute-start.2 = (bf16[192,256]{1,0:T(8,128)(2,1)}, bf16[192,256]{1,0:T(8,128)(2,1)S(1)}, u32[]{:S(2)}, u32[]{:S(2)}) collective-permute-start(bf16[192,256]{1,0:T(8,128)(2,1)} %param.15), channel_id=1, source_target_pairs={{0,2},{1,3},{2,4},{3,5},{4,6},{5,7},{6,32},{7,33},{32,34},{33,35},... | collective-permute-start | bytes 294920 | tf_op jit(solution)/shard_map/ppermute | solution.py:21
  21.6 23.4 %collective-permute-start.1 = (bf16[192,256]{1,0:T(8,128)(2,1)}, bf16[192,256]{1,0:T(8,128)(2,1)S(1)}, u32[]{:S(2)}, u32[]{:S(2)}) collective-permute-start(bf16[192,256]{1,0:T(8,128)(2,1)} %param.16), channel_id=1, source_target_pairs={{0,1},{1,2},{2,3},{3,4},{4,5},{5,6},{6,7},{7,32},{32,33},{33,34},{... | collective-permute-start | bytes 294920 | tf_op jit(solution)/shard_map/ppermute | solution.py:21
  24.6 32.3 %collective-permute-start.5 = (bf16[192,256]{1,0:T(8,128)(2,1)}, bf16[192,256]{1,0:T(8,128)(2,1)S(1)}, u32[]{:S(2)}, u32[]{:S(2)}) collective-permute-start(bf16[192,256]{1,0:T(8,128)(2,1)} %param.16), channel_id=1, source_target_pairs={{0,3},{1,4},{2,5},{3,6},{4,7},{5,32},{6,33},{7,34},{32,35},{33,36}... | collective-permute-start | bytes 294920 | tf_op jit(solution)/shard_map/ppermute | solution.py:21
  31.1 19.5 %collective-permute-start.3 = (bf16[192,256]{1,0:T(8,128)(2,1)}, bf16[192,256]{1,0:T(8,128)(2,1)S(1)}, u32[]{:S(2)}, u32[]{:S(2)}) collective-permute-start(bf16[192,256]{1,0:T(8,128)(2,1)} %param.16), channel_id=1, source_target_pairs={{0,2},{1,3},{2,4},{3,5},{4,6},{5,7},{6,32},{7,33},{32,34},{33,35},... | collective-permute-start | bytes 294920 | tf_op jit(solution)/shard_map/ppermute | solution.py:21
Sparse Core Ops, SparseCore 0:
  104.9 264.5 reduce-scatter.1
where the time goes:
time: 378 us; the launch traced here: 376 us
  waiting for transfers between devices  265 us (70%)
  blocking collectives  26.9 us (7%)
  starting transfers between devices  25.3 us (7%)
  matrix products  24 us (6%)
  between operations  16.1 us (4%)
  other arithmetic  10.6 us (3%)
  local copies, waits for them, and re-layouts  8.59 us (2%)
    reduce_scatter x1, waiting for transfers between devices, on_device(): lax.psum_scatter(jnp.dot(spread, out_weight, preferred_element_type=jnp.f...  265 us
    all_to_all x1, blocking collectives, on_device(): lax.all_to_all(attention, 'wsh', split_axis=1, concat_axis=0, tiled=True)  26.9 us
    ppermute x6, starting transfers between devices, shifted(): return lax.ppermute(block, axis, route)  25.3 us
    dot_general x1, matrix products, on_device(): jnp.dot(spread, out_weight, preferred_element_type=jnp.float32)  13.9 us
  transfers between devices with their start and end apart: 7, of which 1 were waited for; matrix products, arithmetic and copies ran while one was open for 6% of the time, Pallas kernels for 0%

commit v1 on v0

--- a/solution.py
+++ b/solution.py
@@ -83,13 +83,11 @@
     running_max, running_sum, weighted = carried
     normalizer = jnp.transpose(running_sum, (2, 0, 1))[..., None]
     attention = (weighted / normalizer).reshape(row_count, -1).astype(jnp.bfloat16)
-    spread = lax.all_to_all(attention, "wsh", split_axis=1, concat_axis=0, tiled=True)
-    return lax.psum_scatter(
-        jnp.dot(spread, out_weight, preferred_element_type=jnp.float32).astype(jnp.bfloat16),
-        ("head", "wsh"),
-        scatter_dimension=0,
-        tiled=True,
-    )
+    weight_block = lax.all_to_all(out_weight, "wsh", split_axis=1, concat_axis=0, tiled=True)
+    gathered = lax.all_gather(attention, "wsh", axis=0, tiled=True)
+    partial_sum = jnp.dot(gathered, weight_block, preferred_element_type=jnp.float32).astype(jnp.bfloat16)
+    summed = lax.psum_scatter(partial_sum, "head", scatter_dimension=0, tiled=True)
+    return lax.all_to_all(summed, "wsh", split_axis=0, concat_axis=1, tiled=True)
 
 
 def solution(mesh):

time: 378 us -> 318 us (0.84)
  waiting for transfers between devices: 265 us -> 46.1 us
  blocking collectives: 26.9 us -> 180 us
  local copies, waits for them, and re-layouts: 8.59 us -> 22.4 us
  matrix products: 24 us -> 18.9 us
    reduce_scatter x1, waiting for transfers between devices: 265 us -> 39.6 us  [on_device(): lax.psum_scatter(partial_sum, 'head', scatter_dimension=0, tiled=True)]
    all_to_all x1 -> x2, blocking collectives: 26.9 us -> 180 us  [the longest x1 149 us: on_device(): lax.all_to_all(out_weight, 'wsh', split_axis=1, concat_axis=0, tiled=True)]
    unnamed x3 -> x5, local copies, waits for them, and re-layouts: 1.29 us -> 8.78 us
    all_to_all x0 -> x2, local copies, waits for them, and re-layouts: none -> 7.45 us  [the longest x1 6.5 us: on_device(): lax.all_to_all(out_weight, 'wsh', split_axis=1, concat_axis=0, tiled=True)]
    all_gather x0 -> x1, waiting for transfers between devices: none -> 6.37 us  [on_device(): gathered = lax.all_gather(attention, 'wsh', axis=0, tiled=True)]
  transfers between devices with their start and end apart: 7 -> 8, of which waited for: 1 -> 2; matrix products, arithmetic and copies ran while one was open for 6% -> 9% of each run, Pallas kernels for 0% -> 0%
where the time goes in v1:
time: 318 us; the launch traced here: 317 us
  blocking collectives  180 us (57%)
  waiting for transfers between devices  46.1 us (14%)
  starting transfers between devices  25.3 us (8%)
  local copies, waits for them, and re-layouts  22.4 us (7%)
  matrix products  18.9 us (6%)
  between operations  16.1 us (5%)
  other arithmetic  8.2 us (3%)
    all_to_all x1, blocking collectives, on_device(): lax.all_to_all(out_weight, 'wsh', split_axis=1, concat_axis=0, tiled=True)  149 us
    reduce_scatter x1, waiting for transfers between devices, on_device(): lax.psum_scatter(partial_sum, 'head', scatter_dimension=0, tiled=True)  39.6 us
    all_to_all x1, blocking collectives, on_device(): lax.all_to_all(summed, 'wsh', split_axis=0, concat_axis=1, tiled=True)  30 us
    ppermute x6, starting transfers between devices, shifted(): return lax.ppermute(block, axis, route)  25.3 us
    dot_general x1, matrix products, on_device(): jnp.dot(gathered, weight_block, preferred_element_type=jnp.float32)  11.2 us
    unnamed x5, local copies, waits for them, and re-layouts  8.78 us
    all_to_all x1, local copies, waits for them, and re-layouts, on_device(): lax.all_to_all(out_weight, 'wsh', split_axis=1, concat_axis=0, tiled=True)  6.5 us
    all_gather x1, waiting for transfers between devices, on_device(): gathered = lax.all_gather(attention, 'wsh', axis=0, tiled=True)  6.37 us
  transfers between devices with their start and end apart: 8, of which 2 were waited for; matrix products, arithmetic and copies ran while one was open for 9% of the time, Pallas kernels for 0%

profile of v1, /device:TPU:8, one launch (start us, length us, event | category | flops | bytes accessed | tf_op | source)
XLA Modules:
  0.0 316.7 jit_solution(17766499816796878686)
XLA Ops:
  6.5 3.9 %collective-permute-start = (bf16[192,256]{1,0:T(8,128)(2,1)}, bf16[192,256]{1,0:T(8,128)(2,1)S(1)}, u32[]{:S(2)}, u32[]{:S(2)}) collective-permute-start(bf16[192,256]{1,0:T(8,128)(2,1)} %param.15), channel_id=1, source_target_pairs={{0,1},{1,2},{2,3},{3,4},{4,5},{5,6},{6,7},{7,32},{32,33},{33,34},{... | collective-permute-start | bytes 294920 | tf_op jit(solution)/shard_map/ppermute | solution.py:21
  10.5 7.7 %collective-permute-start.4 = (bf16[192,256]{1,0:T(8,128)(2,1)}, bf16[192,256]{1,0:T(8,128)(2,1)S(1)}, u32[]{:S(2)}, u32[]{:S(2)}) collective-permute-start(bf16[192,256]{1,0:T(8,128)(2,1)} %param.15), channel_id=1, source_target_pairs={{0,3},{1,4},{2,5},{3,6},{4,7},{5,32},{6,33},{7,34},{32,35},{33,36}... | collective-permute-start | bytes 294920 | tf_op jit(solution)/shard_map/ppermute | solution.py:21
  18.2 3.4 %collective-permute-start.2 = (bf16[192,256]{1,0:T(8,128)(2,1)}, bf16[192,256]{1,0:T(8,128)(2,1)S(1)}, u32[]{:S(2)}, u32[]{:S(2)}) collective-permute-start(bf16[192,256]{1,0:T(8,128)(2,1)} %param.15), channel_id=1, source_target_pairs={{0,2},{1,3},{2,4},{3,5},{4,6},{5,7},{6,32},{7,33},{32,34},{33,35},... | collective-permute-start | bytes 294920 | tf_op jit(solution)/shard_map/ppermute | solution.py:21
  21.6 2.9 collective-permute-start.1
  24.6 1.9 collective-permute-start.5
  26.5 0.1 constant_dynamic-slice_fusion
  26.6 0.6 fusion.83
  29.7 1.3 copy.87
  31.1 5.3 %collective-permute-start.3 = (bf16[192,256]{1,0:T(8,128)(2,1)}, bf16[192,256]{1,0:T(8,128)(2,1)S(1)}, u32[]{:S(2)}, u32[]{:S(2)}) collective-permute-start(bf16[192,256]{1,0:T(8,128)(2,1)} %param.16), channel_id=1, source_target_pairs={{0,2},{1,3},{2,4},{3,5},{4,6},{5,7},{6,32},{7,33},{32,34},{33,35},... | collective-permute-start | bytes 294920 | tf_op jit(solution)/shard_map/ppermute | solution.py:21
  36.4 0.9 fusion.82
  37.3 7.7 %conditional.4 = (f32[2,8,192]{2,1,0:T(8,128)}, f32[2,8,192]{2,1,0:T(8,128)S(1)}, f32[192,2,8,128]{3,0,2,1:T(8,128)S(1)}) conditional(s32[]{:T(128)} %convert_element_type.38, () %tuple.38, (s32[192]{0:T(256)S(1)}, s32[192]{0:T(256)S(1)}, bf16[192,256]{1,0:T(8,128)(2,1)}, bf16[192,2,8,128]{3,2,1,0:T(8,128)(2,1)S(1)}, bf16[192,256]{1,0:T(8,128)(2,1)}) %tuple.83), branch_computations={%region_0.1_spmd, %region_1.4_spmd} | conditional | flops 310173696 | bytes 10311192 | solution.py:82
  37.3 0.1 fusion.14
  37.4 0.9 reshape.66
  38.3 0.9 reshape.65
  39.3 0.8 fusion
  40.1 0.6 fusion.17
  40.7 1.5 fusion.2
  42.2 2.1 bitcast_add_fusion
  44.3 0.7 fusion.18
  45.1 6.3 %conditional.6 = ((f32[2,8,192]{2,1,0:T(8,128)}, f32[2,8,192]{2,1,0:T(8,128)S(1)}, f32[192,2,8,128]{3,0,2,1:T(8,128)S(1)})) conditional(s32[]{:T(128)} %convert_element_type.36, (f32[2,8,192]{2,1,0:T(8,128)}, f32[2,8,192]{2,1,0:T(8,128)S(1)}, f32[192,2,8,128]{3,0,2,1:T(8,128)S(1)}) %get-tuple-element.317, (s32[192]{0:T(256)S(1)}, s32[]{:T(128)}, ...), branch_computations={%region_8.9_spmd, %region_9.12_spmd} | conditional | flops 310490112 | bytes 11947102 | solution.py:82
  45.1 0.8 dynamic_slice.17
  45.9 0.1 broadcast_compare_fusion.1
  46.0 0.8 fusion.42
  46.9 0.7 fusion.58
  47.6 1.6 bitcast_add_fusion.2
  49.2 0.8 fusion.44
  50.0 0.7 multiply_add_fusion.1
  50.8 0.6 copy.146
  51.4 5.7 %conditional.7 = ((f32[2,8,192]{2,1,0:T(8,128)S(1)}, f32[192,2,8,128]{3,0,2,1:T(8,128)S(1)})) conditional(s32[]{:T(128)} %convert_element_type.35, (f32[2,8,192]{2,1,0:T(8,128)S(1)}, f32[192,2,8,128]{3,0,2,1:T(8,128)S(1)}) %tuple.42, (s32[192]{0:T(256)S(1)}, s32[]{:T(128)}, s32[12288]{0:T(1024)}, bf16[192,256]{1,0:T(8,128)(2,1)S(1)}, ...), branch_computations={%region_12.13_spmd, %region_13.16_spmd} | conditional | flops 310490112 | bytes 11922518 | solution.py:82
  51.4 0.8 dynamic_slice.18
  52.2 0.1 broadcast_compare_fusion.2
  52.3 0.8 fusion.62
  53.1 0.7 fusion.78
  53.9 1.6 bitcast_add_fusion.3
  55.5 0.8 fusion.64
  56.3 0.7 multiply_add_fusion.2
  57.0 0.5 divide_convert_fusion
  57.5 0.5 copy.54
  58.0 1.1 copy.130
  59.2 0.0 reduce-scatter.2.cloned.1.call-start
  59.2 6.4 %copy.55 = bf16[256,8192]{0,1:T(8,128)(2,1)} copy(bf16[256,8192]{1,0:T(8,128)(2,1)} %param.19) | data formatting | bytes 8388608 | tf_op args[5]
  65.6 149.5 %all_to_all.38 = bf16[256,8,1024]{0,2,1:T(8,128)(2,1)} all-to-all(bf16[256,8,1024]{0,2,1:T(8,128)(2,1)} %bitcast.103), channel_id=1, replica_groups=mesh['srv'=8,'head'=4,'wsh'=8] {'wsh'}, dimensions={1} | all-to-all | bytes 8388608 | tf_op jit(solution)/shard_map/all_to_all | solution.py:86
  215.1 6.5 %copy.56 = bf16[8,256,1024]{2,1,0:T(8,128)(2,1)} copy(bf16[8,256,1024]{1,2,0:T(8,128)(2,1)} %bitcast.102) | data formatting | bytes 8388608 | tf_op jit(solution)/shard_map/all_to_all | solution.py:86
  221.6 6.4 %all-gather.2.cloned.1.call-done = bf16[1536,2048]{1,0:T(8,128)(2,1)} async-done(((bf16[192,2048]{1,0:T(8,128)(2,1)}), bf16[1536,2048]{1,0:T(8,128)(2,1)}) %all-gather.2.cloned.1.call-update) | async-done | bytes 6291472 | tf_op jit(solution)/shard_map/all_gather | solution.py:87
  228.0 11.2 %convolution_convert_fusion = bf16[1536,1024]{1,0:T(8,128)(2,1)} fusion(bf16[1536,2048]{1,0:T(8,128)(2,1)} %all-gather.2.cloned.1.call-done, bf16[2048,1024]{1,0:T(8,128)(2,1)} %bitcast.104), kind=kOutput, calls=%fused_computation.94 | convolution fusion | flops 6444023808 | bytes 13631488 | tf_op jit(solution)/shard_map/dot_general | solution.py:88
  239.2 39.6 %reduce-scatter.2.cloned.1.call-done = bf16[384,1024]{1,0:T(8,128)(2,1)} async-done(((bf16[1536,1024]{1,0:T(8,128)(2,1)}), bf16[384,1024]{1,0:T(8,128)(2,1)}) %reduce-scatter.2.cloned.1.call-update) | async-done | bytes 786448 | tf_op jit(solution)/shard_map/reduce_scatter | solution.py:89
  278.8 30.0 %all_to_all.39 = bf16[8,48,1024]{2,1,0:T(8,128)(2,1)S(1)} all-to-all(bf16[8,48,1024]{2,1,0:T(8,128)(2,1)} %bitcast.109), channel_id=1, replica_groups=mesh['srv'=8,'head'=4,'wsh'=8] {'wsh'}, dimensions={0} | all-to-all | bytes 1572864 | tf_op jit(solution)/shard_map/all_to_all | solution.py:90
  308.9 0.9 copy.86
  (16 shorter events, 0.2 us)
Async XLA Ops:
  6.5 20.0 %copy-start = (s32[64,4]{0,1:T(4,128)S(1)}, s32[64,4]{0,1:T(4,128)}, u32[]{:S(2)}) copy-start(s32[64,4]{0,1:T(4,128)} %param.18) | copy-start | bytes 3076
  6.5 221.4 %all-gather.2.cloned.1.call-start = ((), (), s32[]{:S(2)}) async-start(), calls=%async_computation.3 | async-start | bytes 7077888 | tf_op jit(solution)/shard_map/all_gather | solution.py:87
  6.5 24.5 %collective-permute-start = (bf16[192,256]{1,0:T(8,128)(2,1)}, bf16[192,256]{1,0:T(8,128)(2,1)S(1)}, u32[]{:S(2)}, u32[]{:S(2)}) collective-permute-start(bf16[192,256]{1,0:T(8,128)(2,1)} %param.15), channel_id=1, source_target_pairs={{0,1},{1,2},{2,3},{3,4},{4,5},{5,6},{6,7},{7,32},{32,33},{33,34},{... | collective-permute-start | bytes 294920 | tf_op jit(solution)/shard_map/ppermute | solution.py:21
  10.5 40.9 %collective-permute-start.4 = (bf16[192,256]{1,0:T(8,128)(2,1)}, bf16[192,256]{1,0:T(8,128)(2,1)S(1)}, u32[]{:S(2)}, u32[]{:S(2)}) collective-permute-start(bf16[192,256]{1,0:T(8,128)(2,1)} %param.15), channel_id=1, source_target_pairs={{0,3},{1,4},{2,5},{3,6},{4,7},{5,32},{6,33},{7,34},{32,35},{33,36}... | collective-permute-start | bytes 294920 | tf_op jit(solution)/shard_map/ppermute | solution.py:21
  18.2 26.8 %collective-permute-start.2 = (bf16[192,256]{1,0:T(8,128)(2,1)}, bf16[192,256]{1,0:T(8,128)(2,1)S(1)}, u32[]{:S(2)}, u32[]{:S(2)}) collective-permute-start(bf16[192,256]{1,0:T(8,128)(2,1)} %param.15), channel_id=1, source_target_pairs={{0,2},{1,3},{2,4},{3,5},{4,6},{5,7},{6,32},{7,33},{32,34},{33,35},... | collective-permute-start | bytes 294920 | tf_op jit(solution)/shard_map/ppermute | solution.py:21
  21.6 23.4 %collective-permute-start.1 = (bf16[192,256]{1,0:T(8,128)(2,1)}, bf16[192,256]{1,0:T(8,128)(2,1)S(1)}, u32[]{:S(2)}, u32[]{:S(2)}) collective-permute-start(bf16[192,256]{1,0:T(8,128)(2,1)} %param.16), channel_id=1, source_target_pairs={{0,1},{1,2},{2,3},{3,4},{4,5},{5,6},{6,7},{7,32},{32,33},{33,34},{... | collective-permute-start | bytes 294920 | tf_op jit(solution)/shard_map/ppermute | solution.py:21
  24.6 26.8 %collective-permute-start.5 = (bf16[192,256]{1,0:T(8,128)(2,1)}, bf16[192,256]{1,0:T(8,128)(2,1)S(1)}, u32[]{:S(2)}, u32[]{:S(2)}) collective-permute-start(bf16[192,256]{1,0:T(8,128)(2,1)} %param.16), channel_id=1, source_target_pairs={{0,3},{1,4},{2,5},{3,6},{4,7},{5,32},{6,33},{7,34},{32,35},{33,36}... | collective-permute-start | bytes 294920 | tf_op jit(solution)/shard_map/ppermute | solution.py:21
  31.1 14.0 %collective-permute-start.3 = (bf16[192,256]{1,0:T(8,128)(2,1)}, bf16[192,256]{1,0:T(8,128)(2,1)S(1)}, u32[]{:S(2)}, u32[]{:S(2)}) collective-permute-start(bf16[192,256]{1,0:T(8,128)(2,1)} %param.16), channel_id=1, source_target_pairs={{0,2},{1,3},{2,4},{3,5},{4,6},{5,7},{6,32},{7,33},{32,34},{33,35},... | collective-permute-start | bytes 294920 | tf_op jit(solution)/shard_map/ppermute | solution.py:21
  59.2 219.7 %reduce-scatter.2.cloned.1.call-start = ((), (), s32[]{:S(2)}) async-start(), calls=%async_computation.4 | async-start | bytes 3932160 | tf_op jit(solution)/shard_map/reduce_scatter | solution.py:89
Sparse Core Ops, SparseCore 0:
  59.3 168.6 all-gather.1
  239.3 39.4 reduce-scatter.1

commit v2 on v1

v2 whole, which is shorter than its diff:
```python
from functools import partial
import math

import jax
import jax.numpy as jnp
from jax import lax
from jax.experimental import pallas as pl
from jax.experimental.pallas import tpu as pltpu
from jax.sharding import PartitionSpec as P

HEAD_SIZE = 128
SLAB_REACH = 4
MESH = pl.DeviceIdType.MESH

floor_score = -1e30

ROWS = 192
PIECE = 48
KV = 256
HEADS = 16
KBLK = 2048
NBLK = 2048
NQ = 512
CHUNKS = NBLK // NQ
WIN = SLAB_REACH * ROWS


def mod(a, n):
    return lax.rem(a + n, n)


def aligned(i, step):
    return pl.ds(pl.multiple_of(i * step, step), step)


def kernel(
    q_hbm, k_hbm, v_hbm, bias_hbm, w_hbm, out_hbm,
    q, kw, vw, bias, w, a, abuf, cpart, s1, s2, r1, r2, fb,
    load_sem, h_send, h_recv, wm_send, wm_recv, wp_send, wp_recv, wc_send, wc_recv,
    p_send, p_recv, g_send, g_recv, y_send, y_recv, r1_send, r1_recv, r2_send, r2_recv,
    f_send, f_recv, f_local,
):
    srv = lax.axis_index("srv")
    x = lax.axis_index("head")
    z = lax.axis_index("wsh")
    y = lax.div(srv, 2)
    core = lax.rem(srv, 2)
    slab = srv * 8 + z
    ahead, behind = lax.rem(slab + 1, 64), lax.rem(slab + 63, 64)

    def slab_id(s):
        return {"srv": lax.div(s, 8), "wsh": lax.rem(s, 8)}

    def y_id(step):
        return {"srv": lax.rem(y + step, 4) * 2 + core}

    partner = {"srv": y * 2 + 1 - core}

    def x_id(step):
        return {"head": lax.rem(x + step, 4)}

    def z_id(step):
        return {"wsh": lax.rem(z + step, 8)}

    barrier = pltpu.get_barrier_semaphore()
    greeted = [slab_id(ahead), slab_id(behind), partner, x_id(1), x_id(3)]
    greeted += [y_id(step) for step in (1, 2, 3)] + [z_id(step) for step in range(1, 8)]
    for other in greeted:
        pl.semaphore_signal(barrier, inc=1, device_id=other, device_id_type=MESH)
    pl.semaphore_wait(barrier, len(greeted))

    sent = []

    def remote(src, dst, send_sem, recv_sem, device):
        return pltpu.make_async_remote_copy(
            src_ref=src, dst_ref=dst, send_sem=send_sem, recv_sem=recv_sem,
            device_id=device, device_id_type=MESH,
        )

    def send(*args):
        copy = remote(*args)
        copy.start()
        sent.append(copy)

    def halo(step, which):
        own = (k_hbm, v_hbm)[which]
        window = (kw, vw)[which]
        src = own if step == 1 else window.at[pl.ds((step - 1) * ROWS, ROWS)]
        return remote(
            src, window.at[pl.ds(step * ROWS, ROWS)],
            h_send.at[step - 1, which], h_recv.at[step - 1, which], slab_id(ahead),
        )

    def halo_send(step):
        for which in (0, 1):
            if step > 1:
                halo(step - 1, which).wait_recv()
            copy = halo(step, which)
            copy.start()
            sent.append(copy)

    def w_piece(origin, n):
        return w.at[aligned(core * 8 + origin, 128), pl.ds(n * NQ, NQ)]

    def w_msg(down, n, step):
        sems = (wm_send, wm_recv) if down else (wp_send, wp_recv)
        origin = lax.rem(z + (step - 1 if down else 9 - step), 8)
        if step == 1:
            column = pl.multiple_of(y * NBLK + n * NQ, NQ)
            src = w_hbm.at[aligned(core, 128), pl.ds(column, NQ)]
        else:
            src = w_piece(origin, n)
        return remote(
            src, w_piece(origin, n), sems[0].at[n, step - 1], sems[1].at[n, step - 1],
            z_id(7 if down else 1),
        )

    def w_send(down, n, step):
        copy = w_msg(down, n, step)
        copy.start()
        sent.append(copy)

    def w_wait(down, n, step):
        origin = lax.rem(z + (step if down else 8 - step), 8)
        sems = (wm_send, wm_recv) if down else (wp_send, wp_recv)
        remote(
            w_piece(origin, n), w_piece(origin, n), sems[0].at[n, step - 1],
            sems[1].at[n, step - 1], z_id(7 if down else 1),
        ).wait_recv()

    def fm(n, step):
        w_wait(True, n, step)
        if step < 4:
            w_send(True, n, step + 1)

    def fp(n, step):
        w_wait(False, n, step)
        if step < 3:
            w_send(False, n, step + 1)

    def w_cross(n, half):
        block = w.at[aligned(half, 1024), pl.ds(n * NQ, NQ)]
        return remote(block, block, wc_send.at[n], wc_recv.at[n], partner)

    def w_cross_send(n):
        copy = w_cross(n, core)
        copy.start()
        sent.append(copy)

    halo_send(1)
    loads = [
        pltpu.make_async_copy(q_hbm, q, load_sem.at[0]),
        pltpu.make_async_copy(k_hbm, kw.at[pl.ds(0, ROWS)], load_sem.at[1]),
        pltpu.make_async_copy(v_hbm, vw.at[pl.ds(0, ROWS)], load_sem.at[2]),
        pltpu.make_async_copy(bias_hbm, bias, load_sem.at[3]),
        pltpu.make_async_copy(
            w_hbm.at[aligned(core, 128), aligned(y, NBLK)],
            w.at[aligned(core * 8 + z, 128)], load_sem.at[4],
        ),
    ]
    w_send(True, 0, 1)
    w_send(True, 1, 1)
    for load in loads:
        load.start()
    halo_send(2)
    fm(0, 1)
    fm(1, 1)
    halo_send(3)
    w_send(False, 0, 1)
    w_send(False, 1, 1)
    for load in loads:
        load.wait()
    fm(0, 2)
    fm(1, 2)
    halo(3, 0).wait_recv()
    halo(3, 1).wait_recv()

    factor = math.log2(math.e) / math.sqrt(HEAD_SIZE)

    def a_rows(x_dest, y_src):
        return a.at[aligned(x_dest * 4 + y_src, PIECE)]

    def attend(j):
        rows = aligned(j, PIECE)

        def group(g, carry):
            columns = pl.multiple_of(g * HEAD_SIZE, HEAD_SIZE)
            key = kw[:, pl.ds(columns, HEAD_SIZE)]
            value = vw[:, pl.ds(columns, HEAD_SIZE)]
            stacked = jnp.concatenate(
                [
                    q[rows, pl.ds(pl.multiple_of((g * 8 + i) * HEAD_SIZE, HEAD_SIZE), HEAD_SIZE)]
                    for i in range(8)
                ],
                axis=0,
            )
            scores = lax.dot_general(
                stacked, key, (((1,), (1,)), ((), ())), preferred_element_type=jnp.float32
            )
            scores = scores.reshape(8, PIECE, WIN) * factor + bias[rows, :][None]
            terms = jnp.exp2(scores - jnp.max(scores, axis=-1, keepdims=True))
            total = jnp.sum(terms, axis=-1, keepdims=True)
            weighted = jnp.dot(
                terms.astype(jnp.bfloat16).reshape(8 * PIECE, WIN), value,
                preferred_element_type=jnp.float32,
            ).reshape(8, PIECE, HEAD_SIZE)
            result = (weighted / total).astype(jnp.bfloat16)
            for i in range(8):
                place = pl.multiple_of(((i % 2) * 8 + g * 4 + i // 2) * HEAD_SIZE, HEAD_SIZE)
                abuf[rows, pl.ds(place, HEAD_SIZE)] = result[i]
            return carry

        lax.fori_loop(0, 2, group, 0)

    def p_copy(jj, j, dest):
        return remote(
            abuf.at[aligned(j, PIECE)], a_rows(lax.div(z, 2), y),
            p_send.at[jj], p_recv.at[lax.div(z, 2)], {"wsh": dest},
        )

    def p_place(jj):
        j = lax.rem(jj + lax.div(z, 2), 4)
        return j, 4 * lax.rem(z, 2) + j

    def p_start(jj):
        j, dest = p_place(jj)

        @pl.when(dest == z)
        def _():
            pltpu.make_async_copy(
                abuf.at[aligned(j, PIECE)], a_rows(lax.div(z, 2), y), p_recv.at[lax.div(z, 2)]
            ).start()

        @pl.when(dest != z)
        def _():
            p_copy(jj, j, dest).start()

    def p_piece(jj):
        return lax.rem(lax.rem(z, 4) + 4 - jj, 4)

    def p_wait(jj):
        place = a_rows(p_piece(jj), y)
        pltpu.make_async_copy(place, place, p_recv.at[p_piece(jj)]).wait()

    def g_msg(up, jj, y_src):
        place = a_rows(p_piece(jj), y_src)
        d = 0 if up else 1
        return remote(place, place, g_send.at[d, jj], g_recv.at[d, jj], y_id(1 if up else 3))

    def g_start(jj):
        for up in (True, False):
            copy = g_msg(up, jj, y)
            copy.start()
            sent.append(copy)

    def g_wait(up, jj):
        g_msg(up, jj, lax.rem(y + (3 if up else 1), 4)).wait_recv()

    def y_msg(up, jj, y_src):
        place = a_rows(p_piece(jj), y_src)
        return remote(place, place, y_send.at[jj], y_recv.at[jj], y_id(1 if up else 3))

    def y_relay(jj):
        up = jj < 2
        copy = y_msg(up, jj, lax.rem(y + (3 if up else 1), 4))
        copy.start()
        sent.append(copy)

    def y_wait(jj):
        y_msg(jj < 2, jj, lax.rem(y + 2, 4)).wait_recv()

    fp(0, 1)
    for jj in range(4):
        attend(p_place(jj)[0])
        p_start(jj)
        if jj == 0:
            fp(1, 1)
            fm(0, 3)
        if jj == 1:
            fm(1, 3)
            w_send(True, 2, 1)
            w_send(True, 3, 1)
            fp(0, 2)
        if jj == 2:
            fp(1, 2)
            w_send(False, 2, 1)
            w_send(False, 3, 1)
            p_wait(0)
            g_start(0)
            fm(0, 4)
    fm(1, 4)
    p_wait(1)
    g_start(1)
    fp(0, 3)
    w_cross_send(0)
    fp(1, 3)
    w_cross_send(1)
    p_wait(2)
    g_start(2)
    g_wait(True, 0)
    y_relay(0)
    fm(2, 1)
    fm(3, 1)
    p_wait(3)
    g_start(3)
    g_wait(True, 1)
    y_relay(1)
    fp(2, 1)
    fp(3, 1)
    fm(2, 2)
    fm(3, 2)
    g_wait(False, 2)
    y_relay(2)
    g_wait(False, 3)
    y_relay(3)
    fp(2, 2)
    fp(3, 2)
    fm(2, 3)
    fm(3, 3)
    g_wait(False, 0)
    g_wait(False, 1)
    g_wait(True, 2)
    g_wait(True, 3)
    for jj in range(4):
        y_wait(jj)

    def project(n, step):
        rows = a[aligned(lax.rem(x + step, 4), ROWS), :]
        return jnp.dot(rows, w[:, pl.ds(n * NQ, NQ)], preferred_element_type=jnp.float32)

    half = ROWS // 2

    def r1_msg(up, n):
        d = 0 if up else 1
        return remote(
            s1.at[n, pl.ds(d * half, half)], r1.at[n, d],
            r1_send.at[n, d], r1_recv.at[n, d], x_id(1 if up else 3),
        )

    def r2_msg(up, n):
        d = 0 if up else 1
        return remote(
            s2.at[n, d], r2.at[n, d], r2_send.at[n, d], r2_recv.at[n, d], x_id(1 if up else 3)
        )

    def start(copy):
        copy.start()
        sent.append(copy)

    def stage1(n):
        w_cross(n, 1 - core).wait_recv()
        s1[n] = project(n, 2).astype(jnp.bfloat16)
        start(r1_msg(True, n))
        start(r1_msg(False, n))
        for d, step in ((0, 1), (1, 3), (2, 0)):
            cpart[n, d] = project(n, step)

    def stage2(n):
        for d, up in ((0, True), (1, False)):
            r1_msg(up, n).wait_recv()
            part = pl.ds(d * half, half)
            other = pl.ds((1 - d) * half, half)
            s2[n, d, part, :] = (cpart[n, d, part, :] + r1[n, d].astype(jnp.float32)).astype(jnp.bfloat16)
            s2[n, d, other, :] = cpart[n, d, other, :].astype(jnp.bfloat16)
            start(r2_msg(up, n))

    def f_place(n):
        return out_hbm.at[:, pl.ds(pl.multiple_of(y * NBLK + n * NQ, NQ), NQ)]

    def f_msg(n, step):
        return remote(
            fb.at[n, aligned(lax.rem(y + step, 4), PIECE)], f_place(n),
            f_send.at[n, step - 1], f_recv.at[n, step - 1], y_id(step),
        )

    def f_own(n):
        return pltpu.make_async_copy(fb.at[n, aligned(y, PIECE)], f_place(n), f_local.at[n])

    def stage3(n):
        r2_msg(True, n).wait_recv()
        r2_msg(False, n).wait_recv()
        total = cpart[n, 2] + r2[n, 0].astype(jnp.float32) + r2[n, 1].astype(jnp.float32)
        fb[n] = total.astype(jnp.bfloat16)
        for step in (1, 2, 3):
            start(f_msg(n, step))
        f_own(n).start()

    stage1(0)
    stage1(1)
    stage2(0)
    fm(2, 4)
    fm(3, 4)
    fp(2, 3)
    w_cross_send(2)
    fp(3, 3)
    w_cross_send(3)
    stage2(1)
    stage3(0)
    stage1(2)
    stage3(1)
    stage1(3)
    stage2(2)
    stage2(3)
    stage3(2)
    stage3(3)

    for n in range(CHUNKS):
        f_own(n).wait()
        for step in (1, 2, 3):
            source = lax.rem(y + 4 - step, 4)
            place = out_hbm.at[:, pl.ds(pl.multiple_of(source * NBLK + n * NQ, NQ), NQ)]
            remote(
                fb.at[n, aligned(y, PIECE)], place,
                f_send.at[n, step - 1], f_recv.at[n, step - 1], y_id(step),
            ).wait_recv()
    for copy in sent:
        copy.wait_send()
    for jj in range(4):
        j, dest = p_place(jj)

        @pl.when(dest != z)
        def _():
            p_copy(jj, j, dest).wait_send()


def on_device(queries, keys, values, doc_ids, block_mask, out_weight):
    slab = lax.axis_index(("srv", "wsh"))
    docs_query = lax.dynamic_slice_in_dim(doc_ids, slab * ROWS, ROWS)
    mask_row = lax.dynamic_index_in_dim(block_mask, slab, 0, keepdims=False)
    parts = []
    for offset in range(SLAB_REACH):
        source = slab - offset
        docs_key = lax.dynamic_slice_in_dim(doc_ids, jnp.maximum(source, 0) * ROWS, ROWS)
        seen = docs_query[:, None] == docs_key[None, :]
        if offset == 0:
            query_pos = lax.broadcasted_iota(jnp.int32, (ROWS, ROWS), 0)
            key_pos = lax.broadcasted_iota(jnp.int32, (ROWS, ROWS), 1)
            seen = seen & (key_pos <= query_pos)
        parts.append(seen & (mask_row[offset] > 0) & (source >= 0))
    bias = jnp.where(jnp.concatenate(parts, axis=1), 0.0, floor_score).astype(jnp.float32)

    any_space = pl.BlockSpec(memory_space=pl.ANY)
    dma = pltpu.SemaphoreType.DMA
    bf16, f32 = jnp.bfloat16, jnp.float32
    return pl.pallas_call(
        kernel,
        out_shape=jax.ShapeDtypeStruct((PIECE, 4 * NBLK), bf16),
        in_specs=[any_space] * 5,
        out_specs=any_space,
        scratch_shapes=[
            pltpu.VMEM((ROWS, KBLK), bf16),
            pltpu.VMEM((WIN, KV), bf16),
            pltpu.VMEM((WIN, KV), bf16),
            pltpu.VMEM((ROWS, WIN), f32),
            pltpu.VMEM((KBLK, NBLK), bf16),
            pltpu.VMEM((4 * ROWS, KBLK), bf16),
            pltpu.VMEM((ROWS, KBLK), bf16),
            pltpu.VMEM((CHUNKS, 3, ROWS, NQ), f32),
            pltpu.VMEM((CHUNKS, ROWS, NQ), bf16),
            pltpu.VMEM((CHUNKS, 2, ROWS, NQ), bf16),
            pltpu.VMEM((CHUNKS, 2, ROWS // 2, NQ), bf16),
            pltpu.VMEM((CHUNKS, 2, ROWS, NQ), bf16),
            pltpu.VMEM((CHUNKS, ROWS, NQ), bf16),
            dma((5,)),
            dma((3, 2)), dma((3, 2)),
            dma((CHUNKS, 4)), dma((CHUNKS, 4)),
            dma((CHUNKS, 3)), dma((CHUNKS, 3)),
            dma((CHUNKS,)), dma((CHUNKS,)),
            dma((4,)), dma((4,)),
            dma((2, 4)), dma((2, 4)),
            dma((4,)), dma((4,)),
            dma((CHUNKS, 2)), dma((CHUNKS, 2)),
            dma((CHUNKS, 2)), dma((CHUNKS, 2)),
            dma((CHUNKS, 3)), dma((CHUNKS, 3)), dma((CHUNKS,)),
        ],
        compiler_params=pltpu.CompilerParams(
            collective_id=0, has_side_effects=True, vmem_limit_bytes=60 * 1024 * 1024
        ),
    )(queries, keys, values, bias, out_weight)


def solution(mesh):
    in_specs = (
        P(("srv", "wsh"), "head"),
        P(("srv", "wsh"), "head"),
        P(("srv", "wsh"), "head"),
        P(),
        P(),
        P(("head", "wsh"), None),
    )
    out_specs = P(("srv", "head", "wsh"), None)
    return jax.shard_map(
        on_device, mesh=mesh, in_specs=in_specs, out_specs=out_specs, check_vma=False
    )
```

time: 318 us -> 123 us (0.39)
  blocking collectives: 180 us -> 0 us
  Pallas kernels: 0 us -> 114 us
  waiting for transfers between devices: 46.1 us -> 0 us
  starting transfers between devices: 25.3 us -> 0 us
  matrix products: 18.9 us -> 0 us
  local copies, waits for them, and re-layouts: 22.4 us -> 4.4 us
  between operations: 16.1 us -> 2.55 us
  other arithmetic: 8.2 us -> 1.23 us
    all_to_all x2 -> x0, blocking collectives: 180 us -> none  [the longest x1 149 us: on_device(): lax.all_to_all(out_weight, 'wsh', split_axis=1, concat_axis=0, tiled=True)]
    pallas_call x0 -> x1, Pallas kernels: none -> 114 us  [on_device(): pl.pallas_call(kernel, out_shape=jax.ShapeDtypeStruct((PIECE, 4 * NBLK),...]
    reduce_scatter x1 -> x0, waiting for transfers between devices: 39.6 us -> none  [on_device(): lax.psum_scatter(partial_sum, 'head', scatter_dimension=0, tiled=True)]
    ppermute x6 -> x0, starting transfers between devices: 25.3 us -> none  [shifted(): return lax.ppermute(block, axis, route)]
    dot_general x7 -> x0, matrix products: 18.9 us -> none  [the longest x1 11.2 us: on_device(): jnp.dot(gathered, weight_block, preferred_element_type=jnp.float32)]
    all_to_all x2 -> x0, local copies, waits for them, and re-layouts: 7.45 us -> none  [the longest x1 6.5 us: on_device(): lax.all_to_all(out_weight, 'wsh', split_axis=1, concat_axis=0, tiled=True)]
    all_gather x1 -> x0, waiting for transfers between devices: 6.37 us -> none  [on_device(): gathered = lax.all_gather(attention, 'wsh', axis=0, tiled=True)]
    unnamed x5 -> x3, local copies, waits for them, and re-layouts: 8.78 us -> 2.75 us
  transfers between devices with their start and end apart: 8 -> 0, of which waited for: 2 -> 0; matrix products, arithmetic and copies ran while one was open for 9% -> 0% of each run, Pallas kernels for 0% -> 0%
where the time goes in v2:
time: 123 us; the launch traced here: 122 us
  Pallas kernels  114 us (93%)
  local copies, waits for them, and re-layouts  4.4 us (4%)
  between operations  2.55 us (2%)
  other arithmetic  1.23 us (1%)
    pallas_call x1, Pallas kernels, on_device(): pl.pallas_call(kernel, out_shape=jax.ShapeDtypeStruct((PIECE, 4 * NBLK),...  114 us
    unnamed x3, local copies, waits for them, and re-layouts  2.75 us

profile of v2, /device:TPU:8, one launch (start us, length us, event | category | flops | bytes accessed | tf_op | source)
XLA Modules:
  0.0 122.3 jit_solution(1319153728383363166)
XLA Ops:
  0.0 0.0 copy-start
  0.0 0.7 copy-done
  0.7 0.1 constant_dynamic-slice_fusion
  0.8 0.6 fusion.4
  3.9 1.0 fusion.3
  4.9 0.2 fusion.2
  5.1 1.0 add_select_fusion.bias_hbm
  6.1 114.1 %shard_map.64 = bf16[48,8192]{1,0:T(8,128)(2,1)} custom-call(bf16[192,2048]{1,0:T(8,128)(2,1)} %q_hbm.1, bf16[192,256]{1,0:T(8,128)(2,1)} %k_hbm.1, bf16[192,256]{1,0:T(8,128)(2,1)} %v_hbm.1, f32[192,768]{1,0:T(8,128)} %add_select_fusion.bias_hbm, bf16[256,8192]{1,0:T(8,128)(2,1)} %w_hbm.1), custom_call_target="tpu_custom_call" | custom-call | tf_op jit(solution)/shard_map/pallas_call | solution.py:445
  120.2 2.1 %copy.8 = bf16[48,8192]{1,0:T(8,128)(2,1)} copy(bf16[48,8192]{1,0:T(8,128)(2,1)} %shard_map.64) | data formatting | bytes 1572864
Async XLA Ops:
  0.0 0.7 copy-start

commit v3 on v1

v3 whole, which is shorter than its diff:
```python
from functools import partial
import math

import jax
import jax.numpy as jnp
from jax import lax
from jax.experimental import pallas as pl
from jax.experimental.pallas import tpu as pltpu
from jax.sharding import PartitionSpec as P

HEAD_SIZE = 128
SLAB_REACH = 4
MESH = pl.DeviceIdType.MESH

floor_score = -1e30

ROWS = 192
PIECE = 48
KV = 256
HEADS = 16
KBLK = 2048
NBLK = 2048
NQ = 512
CHUNKS = NBLK // NQ
WIN = SLAB_REACH * ROWS
PAIR = 2 * ROWS
PARTS = 3
SUB = PIECE // PARTS


def mod(a, n):
    return lax.rem(a + n, n)


def aligned(i, step):
    return pl.ds(pl.multiple_of(i * step, step), step)


def kernel(
    q_hbm, k_hbm, v_hbm, docs, mask, w_hbm, out_hbm,
    q, kw, vw, bias, peak, acc, w, a, abuf, cpart, s1, s2, r1, r2, fb,
    load_sem, h_send, h_recv, wm_send, wm_recv, wp_send, wp_recv, wc_send, wc_recv,
    p_send, p_recv, g_send, g_recv, y_send, y_recv, r1_send, r1_recv, r2_send, r2_recv,
    f_send, f_recv, f_local,
):
    srv = lax.axis_index("srv")
    x = lax.axis_index("head")
    z = lax.axis_index("wsh")
    y = lax.div(srv, 2)
    core = lax.rem(srv, 2)
    slab = srv * 8 + z
    ahead, behind = lax.rem(slab + 1, 64), lax.rem(slab + 63, 64)

    def slab_id(s):
        return {"srv": lax.div(s, 8), "wsh": lax.rem(s, 8)}

    def y_id(step):
        return {"srv": lax.rem(y + step, 4) * 2 + core}

    partner = {"srv": y * 2 + 1 - core}

    def x_id(step):
        return {"head": lax.rem(x + step, 4)}

    def z_id(step):
        return {"wsh": lax.rem(z + step, 8)}

    barrier = pltpu.get_barrier_semaphore()
    greeted = [slab_id(ahead), slab_id(behind), partner, x_id(1), x_id(3)]
    greeted += [y_id(step) for step in (1, 2, 3)] + [z_id(step) for step in range(1, 8)]
    for other in greeted:
        pl.semaphore_signal(barrier, inc=1, device_id=other, device_id_type=MESH)
    loads = [
        pltpu.make_async_copy(q_hbm, q, load_sem.at[0]),
        pltpu.make_async_copy(k_hbm, kw.at[pl.ds(0, ROWS)], load_sem.at[1]),
        pltpu.make_async_copy(v_hbm, vw.at[pl.ds(0, ROWS)], load_sem.at[2]),
    ]
    for part in (0, 1):
        loads.append(
            pltpu.make_async_copy(
                w_hbm.at[pl.ds(part * 128, 128), aligned(y, NBLK)],
                w.at[aligned(part * 8 + z, 128)], load_sem.at[3 + part],
            )
        )
    for load in loads:
        load.start()

    def docs_of(source):
        first = lax.div(source * 3, 2)
        row, after = docs[pl.ds(first, 1), :], docs[pl.ds(first + 1, 1), :]
        even = jnp.concatenate([row, after[:, :64]], axis=1)
        odd = jnp.concatenate([row[:, 64:], after], axis=1)
        return jnp.where(lax.rem(source, 2) == 0, even, odd).astype(jnp.float32)

    row_ids = lax.broadcasted_iota(jnp.int32, (ROWS, ROWS), 0)
    column_ids = lax.broadcasted_iota(jnp.int32, (ROWS, ROWS), 1)
    docs_query = jnp.sum(
        jnp.where(row_ids == column_ids, docs_of(slab), 0.0), axis=1, keepdims=True
    )
    for offset in range(SLAB_REACH):
        source = slab - offset
        live = (mask[offset, slab] > 0) & (source >= 0)
        seen = docs_query == docs_of(jnp.maximum(source, 0))
        if offset == 0:
            seen = seen & (column_ids <= row_ids)
        bias[:, pl.ds(offset * ROWS, ROWS)] = jnp.where(
            seen, jnp.where(live, 0.0, floor_score), floor_score
        )
    pl.semaphore_wait(barrier, len(greeted))

    sent = []

    def remote(src, dst, send_sem, recv_sem, device):
        return pltpu.make_async_remote_copy(
            src_ref=src, dst_ref=dst, send_sem=send_sem, recv_sem=recv_sem,
            device_id=device, device_id_type=MESH,
        )

    def halo(step, which):
        own = (k_hbm, v_hbm)[which]
        window = (kw, vw)[which]
        src = own if step == 1 else window.at[pl.ds((step - 1) * ROWS, ROWS)]
        return remote(
            src, window.at[pl.ds(step * ROWS, ROWS)],
            h_send.at[step - 1, which], h_recv.at[step - 1, which], slab_id(ahead),
        )

    def halo_send(step):
        for which in (0, 1):
            if step > 1:
                halo(step - 1, which).wait_recv()
            copy = halo(step, which)
            copy.start()
            sent.append(copy)

    def halo_wait():
        halo(3, 0).wait_recv()
        halo(3, 1).wait_recv()

    def w_piece(origin, n):
        return w.at[aligned(core * 8 + origin, 128), pl.ds(n * NQ, NQ)]

    def w_msg(down, n, step):
        sems = (wm_send, wm_recv) if down else (wp_send, wp_recv)
        origin = lax.rem(z + (step - 1 if down else 9 - step), 8)
        if step == 1:
            column = pl.multiple_of(y * NBLK + n * NQ, NQ)
            src = w_hbm.at[aligned(core, 128), pl.ds(column, NQ)]
        else:
            src = w_piece(origin, n)
        return remote(
            src, w_piece(origin, n), sems[0].at[n, step - 1], sems[1].at[n, step - 1],
            z_id(7 if down else 1),
        )

    def w_send(down, n, step):
        copy = w_msg(down, n, step)
        copy.start()
        sent.append(copy)

    def w_wait(down, n, step):
        origin = lax.rem(z + (step if down else 8 - step), 8)
        sems = (wm_send, wm_recv) if down else (wp_send, wp_recv)
        remote(
            w_piece(origin, n), w_piece(origin, n), sems[0].at[n, step - 1],
            sems[1].at[n, step - 1], z_id(7 if down else 1),
        ).wait_recv()

    def w_cross(down, n, step, half):
        origin = lax.rem(z + (step if down else 8 - step), 8)
        block = w.at[aligned(half * 8 + origin, 128), pl.ds(n * NQ, NQ)]
        index = step - 1 if down else step + 3
        return remote(block, block, wc_send.at[n, index], wc_recv.at[n, index], partner)

    def arrive(down, n, step):
        w_wait(down, n, step)
        if step < (4 if down else 3):
            w_send(down, n, step + 1)
        copy = w_cross(down, n, step, core)
        copy.start()
        sent.append(copy)

    def w_complete(n):
        for step in (1, 2, 3, 4):
            w_cross(True, n, step, 1 - core).wait_recv()
        for step in (1, 2, 3):
            w_cross(False, n, step, 1 - core).wait_recv()

    D, U = True, False

    factor = math.log2(math.e) / math.sqrt(HEAD_SIZE)

    def attend(late, part, g):
        place = part * 2 + g
        columns = aligned(g, HEAD_SIZE)
        keys_seen = pl.ds(late * PAIR, PAIR)
        key, value = kw[keys_seen, columns], vw[keys_seen, columns]
        rows = [aligned(j * PARTS + part, SUB) for j in range(4)]
        stacked = jnp.concatenate(
            [q[rows[j], aligned(g * 8 + i, HEAD_SIZE)] for j in range(4) for i in range(8)], axis=0
        )
        scores = lax.dot_general(
            stacked, key, (((1,), (1,)), ((), ())), preferred_element_type=jnp.float32
        )
        scores = jnp.concatenate(
            [
                scores[j * 8 * SUB : (j + 1) * 8 * SUB].reshape(8, SUB, PAIR) * factor
                + bias[rows[j], keys_seen][None]
                for j in range(4)
            ],
            axis=0,
        ).reshape(32 * SUB, PAIR)
        largest = jnp.broadcast_to(jnp.max(scores, axis=-1, keepdims=True), (32 * SUB, HEAD_SIZE))
        if late:
            before = peak[place]
            largest = jnp.maximum(largest, before)
        terms = jnp.exp2(scores - jnp.concatenate([largest] * 3, axis=1)).astype(jnp.bfloat16)
        widened = jnp.concatenate([value, jnp.ones_like(value)], axis=1)
        both = jnp.dot(terms, widened, preferred_element_type=jnp.float32)
        if not late:
            peak[place] = largest
            acc[place] = both
            return
        rescale = jnp.exp2(before - largest)
        both = both + acc[place] * jnp.concatenate([rescale] * 2, axis=1)
        result = (both[:, :HEAD_SIZE] / both[:, HEAD_SIZE:]).astype(jnp.bfloat16)
        for j in range(4):
            for i in range(8):
                abuf[
                    aligned(part * 4 + j, SUB), aligned((i % 2) * 8 + g * 4 + i // 2, HEAD_SIZE)
                ] = result[(j * 8 + i) * SUB : (j * 8 + i + 1) * SUB]

    def attend_early():
        def step(i, carry):
            attend(0, lax.div(i, 2), lax.rem(i, 2))
            return carry

        lax.fori_loop(0, 2 * PARTS, step, 0)

    def attend_late(part):
        def step(g, carry):
            attend(1, part, g)
            return carry

        lax.fori_loop(0, 2, step, 0)

    def p_place(part, x_dest):
        return a.at[aligned((part * 4 + y) * 4 + x_dest, SUB)]

    def p_route(jj):
        j = lax.rem(jj + lax.div(z, 2), 4)
        return j, 4 * lax.rem(z, 2) + j

    def p_copy(part, jj):
        j, dest = p_route(jj)
        return remote(
            abuf.at[aligned(part * 4 + j, SUB)], p_place(part, lax.div(z, 2)),
            p_send.at[part, jj], p_recv.at[part, lax.div(z, 2)], {"wsh": dest},
        )

    def p_start(part):
        for jj in range(4):
            j, dest = p_route(jj)

            @pl.when(dest == z)
            def _():
                pltpu.make_async_copy(
                    abuf.at[aligned(part * 4 + j, SUB)], p_place(part, lax.div(z, 2)),
                    p_recv.at[part, lax.div(z, 2)],
                ).start()

            @pl.when(dest != z)
            def _():
                p_copy(part, jj).start()

    def p_wait(part):
        for x_dest in range(4):
            place = p_place(part, x_dest)
            pltpu.make_async_copy(place, place, p_recv.at[part, x_dest]).wait()

    def start(copy):
        copy.start()
        sent.append(copy)

    def g_msg(d, part, y_src):
        place = a.at[aligned(part * 4 + y_src, 4 * SUB)]
        return remote(place, place, g_send.at[d, part], g_recv.at[d, part], y_id((1, 3)[d]))

    def g_start(part):
        for d in (0, 1):
            start(g_msg(d, part, y))

    def y_msg(d, part, y_src):
        place = a.at[aligned((part * 4 + y_src) * 2 + d, 2 * SUB)]
        return remote(place, place, y_send.at[d, part], y_recv.at[d, part], y_id((1, 3)[d]))

    def y_relay(part):
        for d, back in ((0, 3), (1, 1)):
            source = lax.rem(y + back, 4)
            g_msg(d, part, source).wait_recv()
            start(y_msg(d, part, source))

    def y_wait(part):
        for d in (0, 1):
            y_msg(d, part, lax.rem(y + 2, 4)).wait_recv()

    def owned(x_dest, y_dest):
        return pl.ds(pl.multiple_of((y_dest * 4 + x_dest) * SUB, SUB), SUB)

    def r1_msg(d, part, cols):
        return remote(
            s1.at[part, d, :, cols], r1.at[part, d, :, cols],
            r1_send.at[part, d, cols.start // NQ], r1_recv.at[part, d, cols.start // NQ],
            x_id((1, 3)[d]),
        )

    def r2_msg(d, part, cols):
        return remote(
            s2.at[part, d, :, cols], r2.at[part, d, :, cols],
            r2_send.at[part, d, cols.start // NQ], r2_recv.at[part, d, cols.start // NQ],
            x_id((1, 3)[d]),
        )

    def stage1(part, cols):
        cpart[part, :, cols] = jnp.dot(
            a[pl.ds(part * 16 * SUB, 16 * SUB), :], w[:, cols], preferred_element_type=jnp.float32
        )
        far = lax.rem(x + 2, 4)
        for d in (0, 1):
            for i in (0, 1):
                s1[part, d, pl.ds(i * SUB, SUB), cols] = cpart[
                    part, owned(far, 2 * d + i), cols
                ].astype(jnp.bfloat16)
            start(r1_msg(d, part, cols))

    def stage2(part, cols):
        for d in (0, 1):
            near = lax.rem(x + (1, 3)[d], 4)
            r1_msg(d, part, cols).wait_recv()
            for y_dest in range(4):
                block = cpart[part, owned(near, y_dest), cols]
                if y_dest // 2 == d:
                    got = r1[part, d, pl.ds((y_dest - 2 * d) * SUB, SUB), cols]
                    block = block + got.astype(jnp.float32)
                s2[part, d, pl.ds(y_dest * SUB, SUB), cols] = block.astype(jnp.bfloat16)
            start(r2_msg(d, part, cols))

    def f_msg(part, cols, step, y_src, y_dest):
        column = pl.multiple_of(y_src * NBLK + cols.start, NQ)
        src = fb.at[part, aligned(y_dest, SUB), cols]
        dst = out_hbm.at[pl.ds(part * SUB, SUB), pl.ds(column, cols.size)]
        index = cols.start // NQ
        if step == 0:
            return pltpu.make_async_copy(src, dst, f_local.at[part, index])
        return remote(
            src, dst, f_send.at[part, index, step - 1], f_recv.at[part, index, step - 1], y_id(step)
        )

    def stage3(part, cols):
        for d in (0, 1):
            r2_msg(d, part, cols).wait_recv()
        for y_dest in range(4):
            rows = pl.ds(y_dest * SUB, SUB)
            summed = cpart[part, owned(x, y_dest), cols]
            for d in (0, 1):
                summed = summed + r2[part, d, rows, cols].astype(jnp.float32)
            fb[part, rows, cols] = summed.astype(jnp.bfloat16)
        for step in (1, 2, 3):
            start(f_msg(part, cols, step, y, lax.rem(y + step, 4)))
        f_msg(part, cols, 0, y, y).start()

    halo_send(1)
    w_send(D, 0, 1)
    w_send(D, 1, 1)
    for load in loads:
        load.wait()
    arrive(D, 0, 1)
    halo_send(2)
    arrive(D, 1, 1)
    attend_early()
    halo_send(3)
    w_send(U, 0, 1)
    w_send(U, 1, 1)
    arrive(D, 0, 2)
    arrive(D, 1, 2)
    halo_wait()
    for part in range(PARTS):
        attend_late(part)
        p_start(part)
    n01, n2, n3 = pl.ds(0, 1024), pl.ds(1024, 512), pl.ds(1536, 512)
    p_wait(0)
    g_start(0)
    arrive(U, 0, 1)
    arrive(D, 0, 3)
    p_wait(1)
    g_start(1)
    y_relay(0)
    arrive(U, 1, 1)
    arrive(D, 1, 3)
    p_wait(2)
    g_start(2)
    arrive(U, 0, 2)
    arrive(D, 0, 4)
    w_send(D, 2, 1)
    y_relay(1)
    arrive(U, 1, 2)
    w_send(U, 2, 1)
    arrive(D, 1, 4)
    w_send(D, 3, 1)
    arrive(U, 0, 3)
    y_relay(2)
    arrive(U, 1, 3)
    w_send(U, 3, 1)
    arrive(D, 2, 1)
    w_complete(0)
    w_complete(1)
    y_wait(0)
    stage1(0, n01)
    arrive(U, 2, 1)
    arrive(D, 3, 1)
    arrive(D, 2, 2)
    y_wait(1)
    stage1(1, n01)
    stage2(0, n01)
    arrive(U, 2, 2)
    arrive(U, 3, 1)
    arrive(D, 3, 2)
    y_wait(2)
    stage1(2, n01)
    stage2(1, n01)
    arrive(D, 2, 3)
    arrive(U, 3, 2)
    stage3(0, n01)
    arrive(U, 2, 3)
    arrive(D, 3, 3)
    stage2(2, n01)
    stage3(1, n01)
    arrive(D, 2, 4)
    w_complete(2)
    stage1(0, n2)
    stage3(2, n01)
    stage1(1, n2)
    stage2(0, n2)
    arrive(U, 3, 3)
    stage1(2, n2)
    stage2(1, n2)
    stage3(0, n2)
    arrive(D, 3, 4)
    w_complete(3)
    stage1(0, n3)
    stage2(2, n2)
    stage3(1, n2)
    stage1(1, n3)
    stage2(0, n3)
    stage3(2, n2)
    stage1(2, n3)
    stage2(1, n3)
    stage3(0, n3)
    stage2(2, n3)
    stage3(1, n3)
    stage3(2, n3)

    for cols in (n01, n2, n3):
        for part in range(PARTS):
            f_msg(part, cols, 0, y, y).wait()
            for step in (1, 2, 3):
                f_msg(part, cols, step, lax.rem(y + 4 - step, 4), y).wait_recv()
    for copy in sent:
        copy.wait_send()
    for part in range(PARTS):
        for jj in range(4):

            @pl.when(p_route(jj)[1] != z)
            def _():
                p_copy(part, jj).wait_send()


def on_device(queries, keys, values, doc_ids, block_mask, out_weight):
    any_space = pl.BlockSpec(memory_space=pl.ANY)
    dma = pltpu.SemaphoreType.DMA
    bf16, f32 = jnp.bfloat16, jnp.float32
    return pl.pallas_call(
        kernel,
        out_shape=jax.ShapeDtypeStruct((PIECE, 4 * NBLK), bf16),
        in_specs=[any_space] * 3
        + [pl.BlockSpec(memory_space=pltpu.VMEM), pl.BlockSpec(memory_space=pltpu.SMEM), any_space],
        out_specs=any_space,
        scratch_shapes=[
            pltpu.VMEM((ROWS, KBLK), bf16),
            pltpu.VMEM((WIN, KV), bf16),
            pltpu.VMEM((WIN, KV), bf16),
            pltpu.VMEM((ROWS, WIN), f32),
            pltpu.VMEM((2 * PARTS, 32 * SUB, HEAD_SIZE), f32),
            pltpu.VMEM((2 * PARTS, 32 * SUB, 2 * HEAD_SIZE), f32),
            pltpu.VMEM((KBLK, NBLK), bf16),
            pltpu.VMEM((4 * ROWS, KBLK), bf16),
            pltpu.VMEM((ROWS, KBLK), bf16),
            pltpu.VMEM((PARTS, 16 * SUB, NBLK), f32),
            pltpu.VMEM((PARTS, 2, 2 * SUB, NBLK), bf16),
            pltpu.VMEM((PARTS, 2, 4 * SUB, NBLK), bf16),
            pltpu.VMEM((PARTS, 2, 2 * SUB, NBLK), bf16),
            pltpu.VMEM((PARTS, 2, 4 * SUB, NBLK), bf16),
            pltpu.VMEM((PARTS, 4 * SUB, NBLK), bf16),
            dma((5,)),
            dma((3, 2)), dma((3, 2)),
            dma((CHUNKS, 4)), dma((CHUNKS, 4)),
            dma((CHUNKS, 3)), dma((CHUNKS, 3)),
            dma((CHUNKS, 7)), dma((CHUNKS, 7)),
            dma((PARTS, 4)), dma((PARTS, 4)),
            dma((2, PARTS)), dma((2, PARTS)),
            dma((2, PARTS)), dma((2, PARTS)),
            dma((PARTS, 2, CHUNKS)), dma((PARTS, 2, CHUNKS)),
            dma((PARTS, 2, CHUNKS)), dma((PARTS, 2, CHUNKS)),
            dma((PARTS, CHUNKS, 3)), dma((PARTS, CHUNKS, 3)), dma((PARTS, CHUNKS)),
        ],
        compiler_params=pltpu.CompilerParams(
            collective_id=0, has_side_effects=True, vmem_limit_bytes=60 * 1024 * 1024
        ),
    )(queries, keys, values, doc_ids.reshape(-1, 128), block_mask.T, out_weight)


def solution(mesh):
    in_specs = (
        P(("srv", "wsh"), "head"),
        P(("srv", "wsh"), "head"),
        P(("srv", "wsh"), "head"),
        P(),
        P(),
        P(("head", "wsh"), None),
    )
    out_specs = P(("srv", "head", "wsh"), None)
    return jax.shard_map(
        on_device, mesh=mesh, in_specs=in_specs, out_specs=out_specs, check_vma=False
    )
```

time: 318 us -> 115 us (0.36)
  blocking collectives: 180 us -> 0 us
  Pallas kernels: 0 us -> 111 us
  waiting for transfers between devices: 46.1 us -> 0 us
  starting transfers between devices: 25.3 us -> 0 us
  local copies, waits for them, and re-layouts: 22.4 us -> 2.06 us
  matrix products: 18.9 us -> 0 us
  between operations: 16.1 us -> 0.01 us
  other arithmetic: 8.2 us -> 0 us
    all_to_all x2 -> x0, blocking collectives: 180 us -> none  [the longest x1 149 us: on_device(): lax.all_to_all(out_weight, 'wsh', split_axis=1, concat_axis=0, tiled=True)]
    pallas_call x0 -> x1, Pallas kernels: none -> 111 us  [on_device(): pl.pallas_call(kernel, out_shape=jax.ShapeDtypeStruct((PIECE, 4 * NBLK),...]
    reduce_scatter x1 -> x0, waiting for transfers between devices: 39.6 us -> none  [on_device(): lax.psum_scatter(partial_sum, 'head', scatter_dimension=0, tiled=True)]
    ppermute x6 -> x0, starting transfers between devices: 25.3 us -> none  [shifted(): return lax.ppermute(block, axis, route)]
    dot_general x7 -> x0, matrix products: 18.9 us -> none  [the longest x1 11.2 us: on_device(): jnp.dot(gathered, weight_block, preferred_element_type=jnp.float32)]
    all_to_all x2 -> x0, local copies, waits for them, and re-layouts: 7.45 us -> none  [the longest x1 6.5 us: on_device(): lax.all_to_all(out_weight, 'wsh', split_axis=1, concat_axis=0, tiled=True)]
    unnamed x5 -> x1, local copies, waits for them, and re-layouts: 8.78 us -> 2.06 us
    all_gather x1 -> x0, waiting for transfers between devices: 6.37 us -> none  [on_device(): gathered = lax.all_gather(attention, 'wsh', axis=0, tiled=True)]
  transfers between devices with their start and end apart: 8 -> 0, of which waited for: 2 -> 0; matrix products, arithmetic and copies ran while one was open for 9% -> 0% of each run, Pallas kernels for 0% -> 0%
where the time goes in v3:
time: 115 us; the launch traced here: 113 us
  Pallas kernels  111 us (97%)
  local copies, waits for them, and re-layouts  2.06 us (2%)
    pallas_call x1, Pallas kernels, on_device(): pl.pallas_call(kernel, out_shape=jax.ShapeDtypeStruct((PIECE, 4 * NBLK),...  111 us

profile of v3, /device:TPU:8, one launch (start us, length us, event | category | flops | bytes accessed | tf_op | source)
XLA Modules:
  0.0 113.4 jit_solution(5667745475961255366)
XLA Ops:
  0.0 111.3 %shard_map.64 = bf16[48,8192]{1,0:T(8,128)(2,1)} custom-call(bf16[192,2048]{1,0:T(8,128)(2,1)} %q_hbm.1, bf16[192,256]{1,0:T(8,128)(2,1)} %k_hbm.1, bf16[192,256]{1,0:T(8,128)(2,1)} %v_hbm.1, s32[96,128]{1,0:T(8,128)} %bitcast.2, s32[4,64]{1,0:T(4,128)} %bitcast.3, bf16[256,8192]{1,0:T(8,128)(2,1)} %w_hbm.1), custom_call_target="tpu_custom_call" | custom-call | tf_op jit(solution)/shard_map/pallas_call | solution.py:482
  111.3 2.1 %copy.8 = bf16[48,8192]{1,0:T(8,128)(2,1)} copy(bf16[48,8192]{1,0:T(8,128)(2,1)} %shard_map.64) | data formatting | bytes 1572864

commit v4 on v3

--- a/solution.py
+++ b/solution.py
@@ -13,6 +13,7 @@
 MESH = pl.DeviceIdType.MESH
 
 floor_score = -1e30
+D, U = True, False
 
 ROWS = 192
 PIECE = 48
@@ -20,8 +21,8 @@
 HEADS = 16
 KBLK = 2048
 NBLK = 2048
-NQ = 512
-CHUNKS = NBLK // NQ
+CUTS = (0, 512, 1024, 1536, 1792, NBLK)
+CHUNKS = len(CUTS) - 1
 WIN = SLAB_REACH * ROWS
 PAIR = 2 * ROWS
 PARTS = 3
@@ -34,6 +35,10 @@
 
 def aligned(i, step):
     return pl.ds(pl.multiple_of(i * step, step), step)
+
+
+def chunk(n):
+    return pl.ds(CUTS[n], CUTS[n + 1] - CUTS[n])
 
 
 def kernel(
@@ -138,14 +143,14 @@
         halo(3, 1).wait_recv()
 
     def w_piece(origin, n):
-        return w.at[aligned(core * 8 + origin, 128), pl.ds(n * NQ, NQ)]
+        return w.at[aligned(core * 8 + origin, 128), chunk(n)]
 
     def w_msg(down, n, step):
         sems = (wm_send, wm_recv) if down else (wp_send, wp_recv)
         origin = lax.rem(z + (step - 1 if down else 9 - step), 8)
         if step == 1:
-            column = pl.multiple_of(y * NBLK + n * NQ, NQ)
-            src = w_hbm.at[aligned(core, 128), pl.ds(column, NQ)]
+            column = pl.multiple_of(y * NBLK + CUTS[n], 256)
+            src = w_hbm.at[aligned(core, 128), pl.ds(column, chunk(n).size)]
         else:
             src = w_piece(origin, n)
         return remote(
@@ -168,7 +173,7 @@
 
     def w_cross(down, n, step, half):
         origin = lax.rem(z + (step if down else 8 - step), 8)
-        block = w.at[aligned(half * 8 + origin, 128), pl.ds(n * NQ, NQ)]
+        block = w.at[aligned(half * 8 + origin, 128), chunk(n)]
         index = step - 1 if down else step + 3
         return remote(block, block, wc_send.at[n, index], wc_recv.at[n, index], partner)
 
@@ -185,8 +190,6 @@
             w_cross(True, n, step, 1 - core).wait_recv()
         for step in (1, 2, 3):
             w_cross(False, n, step, 1 - core).wait_recv()
-
-    D, U = True, False
 
     factor = math.log2(math.e) / math.sqrt(HEAD_SIZE)
 
@@ -307,21 +310,24 @@
     def owned(x_dest, y_dest):
         return pl.ds(pl.multiple_of((y_dest * 4 + x_dest) * SUB, SUB), SUB)
 
-    def r1_msg(d, part, cols):
+    def r1_msg(d, part, n):
+        cols = chunk(n)
         return remote(
             s1.at[part, d, :, cols], r1.at[part, d, :, cols],
-            r1_send.at[part, d, cols.start // NQ], r1_recv.at[part, d, cols.start // NQ],
+            r1_send.at[part, d, n], r1_recv.at[part, d, n],
             x_id((1, 3)[d]),
         )
 
-    def r2_msg(d, part, cols):
+    def r2_msg(d, part, n):
+        cols = chunk(n)
         return remote(
             s2.at[part, d, :, cols], r2.at[part, d, :, cols],
-            r2_send.at[part, d, cols.start // NQ], r2_recv.at[part, d, cols.start // NQ],
+            r2_send.at[part, d, n], r2_recv.at[part, d, n],
             x_id((1, 3)[d]),
         )
 
-    def stage1(part, cols):
+    def stage1(part, n):
+        cols = chunk(n)
         cpart[part, :, cols] = jnp.dot(
             a[pl.ds(part * 16 * SUB, 16 * SUB), :], w[:, cols], preferred_element_type=jnp.float32
         )
@@ -331,34 +337,36 @@
                 s1[part, d, pl.ds(i * SUB, SUB), cols] = cpart[
                     part, owned(far, 2 * d + i), cols
                 ].astype(jnp.bfloat16)
-            start(r1_msg(d, part, cols))
-
-    def stage2(part, cols):
+            start(r1_msg(d, part, n))
+
+    def stage2(part, n):
+        cols = chunk(n)
         for d in (0, 1):
             near = lax.rem(x + (1, 3)[d], 4)
-            r1_msg(d, part, cols).wait_recv()
+            r1_msg(d, part, n).wait_recv()
             for y_dest in range(4):
                 block = cpart[part, owned(near, y_dest), cols]
                 if y_dest // 2 == d:
                     got = r1[part, d, pl.ds((y_dest - 2 * d) * SUB, SUB), cols]
                     block = block + got.astype(jnp.float32)
                 s2[part, d, pl.ds(y_dest * SUB, SUB), cols] = block.astype(jnp.bfloat16)
-            start(r2_msg(d, part, cols))
-
-    def f_msg(part, cols, step, y_src, y_dest):
-        column = pl.multiple_of(y_src * NBLK + cols.start, NQ)
+            start(r2_msg(d, part, n))
+
+    def f_msg(part, n, step, y_src, y_dest):
+        cols = chunk(n)
+        column = pl.multiple_of(y_src * NBLK + CUTS[n], 256)
         src = fb.at[part, aligned(y_dest, SUB), cols]
         dst = out_hbm.at[pl.ds(part * SUB, SUB), pl.ds(column, cols.size)]
-        index = cols.start // NQ
         if step == 0:
-            return pltpu.make_async_copy(src, dst, f_local.at[part, index])
+            return pltpu.make_async_copy(src, dst, f_local.at[part, n])
         return remote(
-            src, dst, f_send.at[part, index, step - 1], f_recv.at[part, index, step - 1], y_id(step)
-        )
-
-    def stage3(part, cols):
+            src, dst, f_send.at[part, n, step - 1], f_recv.at[part, n, step - 1], y_id(step)
+        )
+
+    def stage3(part, n):
+        cols = chunk(n)
         for d in (0, 1):
-            r2_msg(d, part, cols).wait_recv()
+            r2_msg(d, part, n).wait_recv()
         for y_dest in range(4):
             rows = pl.ds(y_dest * SUB, SUB)
             summed = cpart[part, owned(x, y_dest), cols]
@@ -366,105 +374,135 @@
                 summed = summed + r2[part, d, rows, cols].astype(jnp.float32)
             fb[part, rows, cols] = summed.astype(jnp.bfloat16)
         for step in (1, 2, 3):
-            start(f_msg(part, cols, step, y, lax.rem(y + step, 4)))
-        f_msg(part, cols, 0, y, y).start()
+            start(f_msg(part, n, step, y, lax.rem(y + step, 4)))
+        f_msg(part, n, 0, y, y).start()
 
     halo_send(1)
     w_send(D, 0, 1)
+    w_send(U, 4, 1)
     w_send(D, 1, 1)
     for load in loads:
         load.wait()
+    w_send(D, 4, 1)
+    halo_send(2)
     arrive(D, 0, 1)
-    halo_send(2)
     arrive(D, 1, 1)
+    w_send(U, 0, 1)
+    halo_send(3)
+    w_send(D, 2, 1)
     attend_early()
-    halo_send(3)
-    w_send(U, 0, 1)
+    arrive(D, 1, 2)
+    w_send(D, 3, 1)
     w_send(U, 1, 1)
+    halo_wait()
+    attend_late(0)
+    p_start(0)
+    attend_late(1)
+    p_start(1)
+    attend_late(2)
+    p_start(2)
+    arrive(D, 4, 1)
     arrive(D, 0, 2)
-    arrive(D, 1, 2)
-    halo_wait()
-    for part in range(PARTS):
-        attend_late(part)
-        p_start(part)
-    n01, n2, n3 = pl.ds(0, 1024), pl.ds(1024, 512), pl.ds(1536, 512)
+    arrive(D, 3, 1)
+    arrive(U, 1, 1)
+    arrive(D, 1, 3)
     p_wait(0)
     g_start(0)
-    arrive(U, 0, 1)
-    arrive(D, 0, 3)
     p_wait(1)
     g_start(1)
+    arrive(D, 4, 2)
     y_relay(0)
-    arrive(U, 1, 1)
-    arrive(D, 1, 3)
+    arrive(U, 0, 1)
     p_wait(2)
     g_start(2)
+    arrive(D, 0, 3)
+    arrive(U, 1, 2)
     arrive(U, 0, 2)
+    y_relay(1)
+    arrive(U, 1, 3)
+    w_send(U, 2, 1)
+    arrive(D, 2, 1)
+    arrive(D, 1, 4)
+    w_send(U, 3, 1)
+    w_complete(1)
+    y_relay(2)
+    arrive(D, 3, 2)
+    y_wait(0)
     arrive(D, 0, 4)
-    w_send(D, 2, 1)
-    y_relay(1)
-    arrive(U, 1, 2)
-    w_send(U, 2, 1)
-    arrive(D, 1, 4)
-    w_send(D, 3, 1)
+    arrive(U, 4, 1)
+    arrive(D, 4, 3)
+    stage1(0, 1)
     arrive(U, 0, 3)
-    y_relay(2)
-    arrive(U, 1, 3)
-    w_send(U, 3, 1)
-    arrive(D, 2, 1)
-    w_complete(0)
-    w_complete(1)
-    y_wait(0)
-    stage1(0, n01)
     arrive(U, 2, 1)
-    arrive(D, 3, 1)
     arrive(D, 2, 2)
     y_wait(1)
-    stage1(1, n01)
-    stage2(0, n01)
+    stage1(1, 1)
+    w_complete(0)
+    stage2(0, 1)
+    arrive(U, 3, 1)
+    stage1(0, 0)
+    stage1(1, 0)
+    arrive(U, 4, 2)
     arrive(U, 2, 2)
-    arrive(U, 3, 1)
-    arrive(D, 3, 2)
     y_wait(2)
-    stage1(2, n01)
-    stage2(1, n01)
+    stage2(1, 1)
     arrive(D, 2, 3)
+    stage1(2, 1)
+    stage1(2, 0)
+    arrive(D, 4, 4)
+    arrive(U, 4, 3)
+    stage2(1, 0)
+    stage2(0, 0)
     arrive(U, 3, 2)
-    stage3(0, n01)
+    arrive(D, 3, 3)
+    w_complete(4)
+    stage1(2, 4)
     arrive(U, 2, 3)
-    arrive(D, 3, 3)
-    stage2(2, n01)
-    stage3(1, n01)
+    stage2(2, 0)
     arrive(D, 2, 4)
+    stage2(2, 1)
+    stage1(1, 4)
+    arrive(U, 3, 3)
+    stage3(1, 0)
     w_complete(2)
-    stage1(0, n2)
-    stage3(2, n01)
-    stage1(1, n2)
-    stage2(0, n2)
-    arrive(U, 3, 3)
-    stage1(2, n2)
-    stage2(1, n2)
-    stage3(0, n2)
     arrive(D, 3, 4)
+    stage1(1, 2)
+    stage2(2, 4)
+    stage1(0, 4)
     w_complete(3)
-    stage1(0, n3)
-    stage2(2, n2)
-    stage3(1, n2)
-    stage1(1, n3)
-    stage2(0, n3)
-    stage3(2, n2)
-    stage1(2, n3)
-    stage2(1, n3)
-    stage3(0, n3)
-    stage2(2, n3)
-    stage3(1, n3)
-    stage3(2, n3)
-
-    for cols in (n01, n2, n3):
+    stage1(1, 3)
+    stage1(0, 2)
+    stage2(1, 2)
+    stage1(2, 2)
+    stage1(0, 3)
+    stage2(0, 2)
+    stage2(0, 4)
+    stage3(0, 1)
+    stage3(1, 1)
+    stage3(2, 1)
+    stage2(1, 4)
+    stage1(2, 3)
+    stage2(0, 3)
+    stage3(1, 2)
+    stage3(0, 2)
+    stage2(2, 2)
+    stage2(1, 3)
+    stage3(2, 4)
+    stage3(1, 4)
+    stage3(2, 0)
+    stage3(0, 0)
+    stage2(2, 3)
+    stage3(0, 4)
+    stage3(0, 3)
+    stage3(2, 2)
+    stage3(1, 3)
+    stage3(2, 3)
+
+    for n in range(CHUNKS):
         for part in range(PARTS):
-            f_msg(part, cols, 0, y, y).wait()
+            f_msg(part, n, 0, y, y).wait()
             for step in (1, 2, 3):
-                f_msg(part, cols, step, lax.rem(y + 4 - step, 4), y).wait_recv()
+                f_msg(part, n, step, lax.rem(y + 4 - step, 4), y).wait_recv()
     for copy in sent:
         copy.wait_send()
     for part in range(PARTS):

time: 115 us -> 108 us (0.939)
  Pallas kernels: 111 us -> 105 us
    pallas_call x1, Pallas kernels: 111 us -> 105 us  [on_device(): pl.pallas_call(kernel, out_shape=jax.ShapeDtypeStruct((PIECE, 4 * NBLK),...]
where the time goes in v4:
time: 108 us; the launch traced here: 107 us
  Pallas kernels  105 us (97%)
  local copies, waits for them, and re-layouts  2.06 us (2%)
    pallas_call x1, Pallas kernels, on_device(): pl.pallas_call(kernel, out_shape=jax.ShapeDtypeStruct((PIECE, 4 * NBLK),...  105 us

profile of v4, /device:TPU:8, one launch (start us, length us, event | category | flops | bytes accessed | tf_op | source)
XLA Modules:
  0.0 107.2 jit_solution(16096168285634037501)
XLA Ops:
  0.0 105.2 %shard_map.64 = bf16[48,8192]{1,0:T(8,128)(2,1)} custom-call(bf16[192,2048]{1,0:T(8,128)(2,1)} %q_hbm.1, bf16[192,256]{1,0:T(8,128)(2,1)} %k_hbm.1, bf16[192,256]{1,0:T(8,128)(2,1)} %v_hbm.1, s32[96,128]{1,0:T(8,128)} %bitcast.2, s32[4,64]{1,0:T(4,128)} %bitcast.3, bf16[256,8192]{1,0:T(8,128)(2,1)} %w_hbm.1), custom_call_target="tpu_custom_call" | custom-call | tf_op jit(solution)/shard_map/pallas_call | solution.py:520
  105.2 2.1 %copy.8 = bf16[48,8192]{1,0:T(8,128)(2,1)} copy(bf16[48,8192]{1,0:T(8,128)(2,1)} %shard_map.64) | data formatting | bytes 1572864

commit v5 on v4

--- a/solution.py
+++ b/solution.py
@@ -519,10 +519,10 @@
     bf16, f32 = jnp.bfloat16, jnp.float32
     return pl.pallas_call(
         kernel,
-        out_shape=jax.ShapeDtypeStruct((PIECE, 4 * NBLK), bf16),
+        out_shape=pltpu.VMEM((PIECE, 4 * NBLK), bf16),
         in_specs=[any_space] * 3
         + [pl.BlockSpec(memory_space=pltpu.VMEM), pl.BlockSpec(memory_space=pltpu.SMEM), any_space],
-        out_specs=any_space,
+        out_specs=pl.BlockSpec(memory_space=pltpu.VMEM),
         scratch_shapes=[
             pltpu.VMEM((ROWS, KBLK), bf16),
             pltpu.VMEM((WIN, KV), bf16),

time: 108 us -> 106 us (0.981)
  local copies, waits for them, and re-layouts: 2.06 us -> 0.88 us
    unnamed x1, local copies, waits for them, and re-layouts: 2.06 us -> 0.88 us
where the time goes in v5:
time: 106 us
  Pallas kernels  105 us (99%)
    pallas_call x1, Pallas kernels, on_device(): pl.pallas_call(kernel, out_shape=pltpu.VMEM((PIECE, 4 * NBLK), bf16), in_...  105 us

profile of v5, /device:TPU:8, one launch (start us, length us, event | category | flops | bytes accessed | tf_op | source)
XLA Modules:
  0.0 106.0 jit_solution(18113233941647061097)
XLA Ops:
  0.0 105.1 %shard_map.64 = bf16[48,8192]{1,0:T(8,128)(2,1)S(1)} custom-call(bf16[192,2048]{1,0:T(8,128)(2,1)} %q_hbm.1, bf16[192,256]{1,0:T(8,128)(2,1)} %k_hbm.1, bf16[192,256]{1,0:T(8,128)(2,1)} %v_hbm.1, s32[96,128]{1,0:T(8,128)} %bitcast.2, s32[4,64]{1,0:T(4,128)} %bitcast.3, bf16[256,8192]{1,0:T(8,128)(2,1)} %w_hbm.1), custom_call_target="tpu_custom_call" | custom-call | tf_op jit(solution)/shard_map/pallas_call | solution.py:520
  105.1 0.9 copy.8
